TPU v7x, 512 devices: a whole 4x8x8 slice. The times are simulated.
512 devices in a mesh: seq: 64 (over z, y), head: 8 (over x, core).
Axes of the slice: x: 4, y: 8, z: 8, core: 2. Of those that a mesh axis runs over, the one named last changes fastest.
Arguments:
- queries: bfloat16 [9216, 8192], P('seq', 'head'), may hold values from -24 to 24
- key_matrix: bfloat16 [9216, 1024], P('seq', 'head'), may hold values from -4 to 4
- value_matrix: bfloat16 [9216, 1024], P('seq', 'head'), may hold values from -6 to 6
- query_feature_weight: bfloat16 [128, 4096], P(None, 'head'), may hold values from -0.5 to 0.5
- key_feature_weight: bfloat16 [128, 512], P(None, 'head'), may hold values from -0.5 to 0.5
Outputs:
- student_out: bfloat16 [9216, 8192], P('seq', 'head')
- query_map_grad: float32 [128, 4096], P(None, 'head')
- key_weight_gradient: float32 [128, 512], P(None, 'head')
- transfer_loss: float32 [], replicated
All inputs are finite; a program needn't handle non-finite values.
Results may differ from a plain program's by a relative error of at most 0.008.
Values may be sent and summed in bfloat16 or wider, within the bound.
A program may use at most 128 MiB of HBM per device.

v0:
```python
import jax
import jax.numpy as jnp
from jax import lax
from jax.sharding import PartitionSpec as P

HEAD_SIZE = 128
GROUP_QUERIES = 8
HALF_FEATURES = 64
NEG_LARGE = -1e30


def prefix(shard, axis, join, neutral, backward):
    count = lax.axis_size(axis)
    place = lax.axis_index(axis)
    ahead = count - 1 - place if backward else place
    gathered = jax.tree.map(
        lambda a, kind: lax.all_gather(a.astype(kind), axis), shard, (jnp.bfloat16, jnp.bfloat16)
    )
    state = jax.tree.map(lambda a, e: jnp.zeros_like(a) + jnp.asarray(e, a.dtype), shard, neutral)

    def one(lap, state):
        source = count - 1 - lap if backward else lap
        return join(
            state,
            jax.tree.map(
                lambda a, own: lax.dynamic_index_in_dim(a, source, 0, False).astype(own.dtype),
                gathered,
                shard,
            ),
        )

    return lax.fori_loop(0, ahead, one, state)


def feature_pair(logits):
    plus_half = jax.nn.softmax(logits, axis=-1)
    minus_half = jax.nn.softmax(-logits, axis=-1)
    return (plus_half, minus_half)


def pair_backward(plus_half, minus_half, d_features):
    feat_count = plus_half.shape[-1]
    d_plus = d_features[..., :feat_count]
    d_minus = d_features[..., feat_count:]
    inner_plus = jnp.sum(d_plus * plus_half, axis=-1, keepdims=True)
    inner_minus = jnp.sum(d_minus * minus_half, axis=-1, keepdims=True)
    return plus_half * (d_plus - inner_plus) - minus_half * (d_minus - inner_minus)


def add_pair(earlier_pair, later_pair):
    return (earlier_pair[0] + later_pair[0], earlier_pair[1] + later_pair[1])


def attend(running, row_block, query_pos, key_view, value_view, key_pos, score_scale):
    row_max, row_sum, weighted = running
    scores = (
        jnp.einsum("rkgd,lkd->kgrl", row_block, key_view, preferred_element_type=jnp.float32)
        * score_scale
    )
    visible = key_pos[None, None, None, :] <= query_pos[None, None, :, None]
    masked = jnp.where(visible, scores, NEG_LARGE)
    new_max = jnp.maximum(row_max, jnp.max(masked, axis=-1))
    exponent = jnp.where(visible, jnp.exp(masked - new_max[..., None]), 0.0)
    weights = exponent.astype(jnp.bfloat16)
    weighted = jnp.einsum("kgrl,lkd->kgrd", weights, value_view, preferred_element_type=jnp.float32)
    row_sum = jnp.sum(exponent, axis=-1)
    return (new_max, row_sum, weighted)


def local(queries, key_matrix, value_matrix, query_feature_weight, key_feature_weight):
    token_rows = queries.shape[0]
    local_heads = key_matrix.shape[1] // HEAD_SIZE
    seq_count = lax.axis_size("seq")
    position = lax.axis_index("seq")
    first_row = position * token_rows
    seg_total = token_rows * seq_count
    score_scale = HEAD_SIZE ** (-0.5)
    query_heads = queries.reshape(token_rows, local_heads, GROUP_QUERIES, HEAD_SIZE)
    key_heads = key_matrix.reshape(token_rows, local_heads, HEAD_SIZE)
    value_heads = value_matrix.reshape(token_rows, local_heads, HEAD_SIZE)
    query_map_view = query_feature_weight.reshape(
        HEAD_SIZE, local_heads, GROUP_QUERIES, HALF_FEATURES
    )
    key_map_view = key_feature_weight.reshape(HEAD_SIZE, local_heads, HALF_FEATURES)
    query_sets = ((query_heads, first_row + jnp.arange(token_rows, dtype=jnp.int32)),)

    def fresh_carry(row_block):
        row_count = row_block.shape[0]
        return (
            jnp.full((local_heads, GROUP_QUERIES, row_count), NEG_LARGE, jnp.float32),
            jnp.zeros((local_heads, GROUP_QUERIES, row_count), jnp.float32),
            jnp.zeros((local_heads, GROUP_QUERIES, row_count, HEAD_SIZE), jnp.float32),
        )

    first_key = jnp.int32(0)
    key_block = lax.all_gather(key_matrix, "seq", axis=0, tiled=True)
    value_block = lax.all_gather(value_matrix, "seq", axis=0, tiled=True)
    key_count = key_block.shape[0]
    key_view = key_block.reshape(key_count, local_heads, HEAD_SIZE)
    value_view = value_block.reshape(key_count, local_heads, HEAD_SIZE)
    key_pos = jnp.arange(key_count, dtype=jnp.int32)
    teach_runs = tuple((fresh_carry(query_set[0]) for query_set in query_sets))
    updated = []
    for query_set, fold_teach_run in zip(query_sets, teach_runs):
        row_block, query_pos = query_set

        def visit_block(current, row_block=row_block, query_pos=query_pos):
            return attend(current, row_block, query_pos, key_view, value_view, key_pos, score_scale)

        def unchanged(current):
            return current

        updated.append(lax.cond(first_key <= query_pos[-1], visit_block, unchanged, fold_teach_run))
    teach_done = tuple(updated)

    def finish(teach_run):
        return (teach_run[2] / teach_run[1][..., None]).astype(jnp.bfloat16)

    finished = [finish(teach_run) for teach_run in teach_done]
    teacher = finished[0]
    query_logits = jnp.einsum(
        "tkgd,dkgf->kgtf", query_heads, query_map_view, preferred_element_type=jnp.float32
    )
    query_plus, query_minus = feature_pair(query_logits)
    query_phi = jnp.concatenate([query_plus, query_minus], axis=-1).astype(jnp.bfloat16)
    logits = jnp.einsum("lkd,dkf->klf", key_heads, key_map_view, preferred_element_type=jnp.float32)
    plus_half, minus_half = feature_pair(logits)
    key_phi = jnp.concatenate([plus_half, minus_half], axis=-1).astype(jnp.bfloat16)
    block_state = jnp.einsum(
        "ktf,tkd->kfd", key_phi, value_heads, preferred_element_type=jnp.float32
    )
    block_norm = jnp.sum(key_phi.astype(jnp.float32), axis=1)
    zero_pair = (jnp.zeros_like(block_state), jnp.zeros_like(block_norm))
    prefix_state, prefix_norm = prefix((block_state, block_norm), "seq", add_pair, zero_pair, False)
    prefix_low = prefix_state.astype(jnp.bfloat16)
    token_index = jnp.arange(token_rows, dtype=jnp.int32)
    causal = token_index[None, :] <= token_index[:, None]
    intra_scores = jnp.where(
        causal,
        jnp.einsum("kgtf,ksf->kgts", query_phi, key_phi, preferred_element_type=jnp.float32),
        0.0,
    )
    numerator = jnp.einsum(
        "kgts,skd->kgtd",
        intra_scores.astype(jnp.bfloat16),
        value_heads,
        preferred_element_type=jnp.float32,
    )
    numerator = numerator + jnp.einsum(
        "kgtf,kfd->kgtd", query_phi, prefix_low, preferred_element_type=jnp.float32
    )
    query_wide = query_phi.astype(jnp.float32)
    denominator = jnp.sum(intra_scores, axis=-1) + jnp.einsum(
        "kgtf,kf->kgt", query_wide, prefix_norm, precision=lax.Precision.HIGHEST
    )
    student = numerator / denominator[..., None]
    target = teacher.astype(jnp.float32)
    differ = student - target
    loss_local = jnp.sum(differ * differ)
    grad_out = 2.0 * differ / seg_total
    numer_grad = grad_out / denominator[..., None]
    denom_grad = -jnp.sum(grad_out * student, axis=-1) / denominator
    numer_low = numer_grad.astype(jnp.bfloat16)
    coupling = (
        jnp.einsum("kgtd,skd->kgts", numer_low, value_heads, preferred_element_type=jnp.float32)
        + denom_grad[..., None]
    )
    coupling_low = jnp.where(causal, coupling, 0.0).astype(jnp.bfloat16)
    later_state = jnp.einsum(
        "kgtf,kgtd->kfd", query_phi, numer_low, preferred_element_type=jnp.float32
    )
    later_norm = jnp.einsum("kgtf,kgt->kf", query_wide, denom_grad, precision=lax.Precision.HIGHEST)
    zero_later = (jnp.zeros_like(later_state), jnp.zeros_like(later_norm))
    suffix_state, suffix_norm = prefix((later_state, later_norm), "seq", add_pair, zero_later, True)
    suffix_low = suffix_state.astype(jnp.bfloat16)
    query_dphi = jnp.einsum(
        "kgts,ksf->kgtf", coupling_low, key_phi, preferred_element_type=jnp.float32
    )
    query_dphi = query_dphi + jnp.einsum(
        "kgtd,kfd->kgtf", numer_low, prefix_low, preferred_element_type=jnp.float32
    )
    query_dphi = query_dphi + denom_grad[..., None] * prefix_norm[:, None, None, :]
    key_dphi = jnp.einsum(
        "kgts,kgtf->ksf", coupling_low, query_phi, preferred_element_type=jnp.float32
    )
    key_dphi = key_dphi + jnp.einsum(
        "skd,kfd->ksf", value_heads, suffix_low, preferred_element_type=jnp.float32
    )
    key_dphi = key_dphi + suffix_norm[:, None, :]
    query_dlogit = pair_backward(query_plus, query_minus, query_dphi).astype(jnp.bfloat16)
    key_dlogit = pair_backward(plus_half, minus_half, key_dphi).astype(jnp.bfloat16)
    query_grad = jnp.einsum(
        "tkgd,kgtf->dkgf", query_heads, query_dlogit, preferred_element_type=jnp.float32
    )
    key_grad = jnp.einsum("tkd,ktf->dkf", key_heads, key_dlogit, preferred_element_type=jnp.float32)
    query_grad, key_grad = lax.psum((query_grad, key_grad), "seq")
    transfer_loss = lax.psum(loss_local, ("seq", "head")) / seg_total
    student_out = (
        student.astype(jnp.bfloat16)
        .transpose(2, 0, 1, 3)
        .reshape(token_rows, local_heads * GROUP_QUERIES * HEAD_SIZE)
    )
    return (
        student_out,
        query_grad.reshape(HEAD_SIZE, local_heads * GROUP_QUERIES * HALF_FEATURES),
        key_grad.reshape(HEAD_SIZE, local_heads * HALF_FEATURES),
        transfer_loss,
    )


def solution(mesh):
    placed = (
        P("seq", "head"),
        P("seq", "head"),
        P("seq", "head"),
        P(None, "head"),
        P(None, "head"),
    )
    return jax.shard_map(
        local,
        mesh=mesh,
        in_specs=placed,
        out_specs=(P("seq", "head"), P(None, "head"), P(None, "head"), P()),
        check_vma=False,
    )
```

profile of v0, /device:TPU:2, one launch (start us, length us, event | category | flops | bytes accessed | tf_op | source)
XLA Modules:
  0.0 812.8 jit_solution(13775298181172924217)
XLA Ops:
  7.9 0.9 fusion.99
  8.9 1.5 convolution_convert_fusion
  13.4 1.0 copy.51
  14.5 49.8 %all-gather.4 = bf16[64,1,128]{2,1,0:T(2,128)(2,1)S(1)} all-gather(bf16[1,1,128]{2,1,0:T(2,128)(2,1)S(1)} %bitcast.271), channel_id=3, replica_groups=mesh['seq'=64,'head'=8] {'seq'}, dimensions={0}, use_global_device_ids=true | all-gather | bytes 16640 | tf_op jit(solution)/shard_map/all_gather | solution.py:17
  64.3 1.3 fusion.103
  65.7 1.3 fusion.100
  67.5 1.1 fusion.38
  68.7 31.2 %all-gather.15.cloned.1.call-done = bf16[8192,128]{1,0:T(8,128)(2,1)} async-done(((bf16[128,128]{1,0:T(8,128)(2,1)}), bf16[8192,128]{1,0:T(8,128)(2,1)}) %all-gather.15.cloned.1.call-update) | async-done | bytes 2097168 | tf_op jit(solution)/shard_map/all_gather | solution.py:17
  100.2 83.5 %all-gather.11.cloned.1.call-done = bf16[9216,128]{1,0:T(8,128)(2,1)} async-done(((bf16[144,128]{1,0:T(8,128)(2,1)}), bf16[9216,128]{1,0:T(8,128)(2,1)}) %all-gather.11.cloned.1.call-update) | async-done | bytes 2359312 | tf_op jit(solution)/shard_map/all_gather | solution.py:96
  183.7 83.7 %all-gather.13.cloned.1.call-done = bf16[9216,128]{1,0:T(8,128)(2,1)} async-done(((bf16[144,128]{1,0:T(8,128)(2,1)}), bf16[9216,128]{1,0:T(8,128)(2,1)}) %all-gather.13.cloned.1.call-update) | async-done | bytes 2359312 | tf_op jit(solution)/shard_map/all_gather | solution.py:97
  267.4 62.5 %conditional.1 = (f32[1,8,144]{2,1,0:T(8,128)}, f32[1,8,144,128]{3,2,1,0:T(8,128)}) conditional(s32[]{:T(128)} %bitcast.28, () %tuple.33, (s32[9216]{0:T(1024)S(1)}, s32[144]{0:T(256)}, bf16[144,1024]{1,0:T(8,128)(2,1)}, bf16[9216,128]{1,0:T(8,128)(2,1)}, bf16[9216,128]{1,0:T(8,128)(2,1)}) %tuple.98), branch_computations={%region_12.13_spmd, %region_13.16_spmd} | conditional | flops 5575162880 | bytes 138378832 | solution.py:113
  267.6 1.4 broadcast_compare_fusion
  269.0 18.7 %fusion = (f32[8,144]{1,0:T(8,128)S(1)}, f32[9216,144,8]{0,1,2:T(8,128)}) fusion(pred[144,9216]{1,0:T(8,128)(4,1)S(1)} %broadcast_compare_fusion, bf16[9216,128]{1,0:T(8,128)(2,1)} %get-tuple-element.118, bf16[144,1024]{1,0:T(8,128)(2,1)} %get-tuple-element.119), kind=kOutput, calls=%fused_computation.4 | convolution fusion | flops 2749758464 | bytes 46453248 | tf_op jit(solution)/shard_map/cond/branch_1_fun/rkgd,lkd->kgrl/dot_general | solution.py:57
  287.7 21.9 %fusion.2 = f32[8,144]{1,0:T(8,128)} fusion(f32[9216,144,8]{0,1,2:T(8,128)} %get-tuple-element.217, f32[8,144]{1,0:T(8,128)S(1)} %broadcast_maximum_fusion, pred[144,9216]{1,0:T(8,128)(4,1)S(1)} %broadcast_compare_fusion), kind=kLoop, calls=%fused_computation.6 | loop fusion | flops 53083008 | bytes 43803648 | tf_op jit(solution)/shard_map/cond/branch_1_fun/reduce_sum | solution.py:66
  309.6 20.2 %fusion.10 = f32[1,8,144,128]{3,2,1,0:T(8,128)} fusion(bf16[9216,128]{1,0:T(8,128)(2,1)} %get-tuple-element.120, f32[9216,144,8]{0,1,2:T(8,128)} %get-tuple-element.217, f32[8,144]{1,0:T(8,128)S(1)} %broadcast_maximum_fusion, pred[144,9216]{1,0:T(8,128)(4,1)S(1)} %broadcast_compare_fusion), kind=kOutput, calls=%fused_computation.14 | convolution fusion | flops 2770993152 | bytes 46748160 | tf_op jit(solution)/shard_map/cond/branch_1_fun/kgrl,lkd->kgrd/dot_general | solution.py:65
  329.9 2.8 multiply_reduce_fusion
  332.9 1.9 fusion.34
  334.9 95.5 %psum.23 = f32[]{:T(128)} all-reduce(f32[]{:T(128)} %get-tuple-element.183), channel_id=1, replica_groups=mesh['seq'=64,'head'=8] {'seq','head'}, use_global_device_ids=true, to_apply=%region_26.27 | all-reduce | flops 1 | bytes 8 | tf_op jit(solution)/shard_map/psum | solution.py:197
  432.8 0.8 copy.65
  434.1 42.6 %all-gather.5 = bf16[64,1,128]{2,1,0:T(2,128)(2,1)S(1)} all-gather(bf16[1,1,128]{2,1,0:T(2,128)(2,1)S(1)} %fusion.36), channel_id=5, replica_groups=mesh['seq'=64,'head'=8] {'seq'}, dimensions={0}, use_global_device_ids=true | all-gather | bytes 16640 | tf_op jit(solution)/shard_map/all_gather | solution.py:17
  477.8 51.3 %while.27 = (s32[]{:T(128)}, f32[1,128,128]{2,1,0:T(8,128)S(1)}, f32[1,128]{1,0:T(1,128)S(1)}, s32[]{:T(128)}, bf16[64,1,128,128]{3,2,1,0:T(8,128)(2,1)}, /*inde...) while((s32[]{:T(128)}, f32[1,128,128]{2,1,0:T(8,128)S(1)}, ...), condition=%wide.region_21.22_spmd, body=%wide.region_20.21_spmd.sunk | while | flops 33030 | bytes 165283 | solution.py:32
  483.5 0.8 convert_add_fusion.10
  484.3 0.8 convert_add_fusion.10
  490.0 0.8 convert_add_fusion.10
  490.8 0.8 convert_add_fusion.10
  494.9 0.8 convert_add_fusion.10
  495.7 0.8 convert_add_fusion.10
  498.2 0.8 convert_add_fusion.10
  499.0 0.8 convert_add_fusion.10
  501.4 0.8 convert_add_fusion.10
  529.5 274.0 %psum.22 = f32[128,64]{0,1:T(8,128)} all-reduce(f32[128,64]{0,1:T(8,128)S(1)} %convolution_bitcast_fusion.3), channel_id=1, replica_groups=mesh['seq'=64,'head'=8] {'seq'}, use_global_device_ids=true, to_apply=%region_24.25 | all-reduce | flops 8192 | bytes 65536 | tf_op jit(solution)/shard_map/psum | solution.py:196
  803.5 1.7 copy.144
  (187 shorter events, 50.6 us)
Async XLA Ops:
  7.2 0.7 copy-start
  7.2 92.6 %all-gather.15.cloned.1.call-start = ((), (), s32[]{:S(2)}) async-start(), calls=%async_computation.3 | async-start | bytes 2129920 | tf_op jit(solution)/shard_map/all_gather | solution.py:17
  8.8 4.5 copy-start.5
  8.9 4.4 copy-start.7
  8.9 4.4 copy-start.9
  10.5 173.1 %all-gather.11.cloned.1.call-start = ((), (), s32[]{:S(2)}) async-start(), calls=%async_computation | async-start | bytes 2396160 | tf_op jit(solution)/shard_map/all_gather | solution.py:96
  11.3 256.1 %all-gather.13.cloned.1.call-start = ((), (), s32[]{:S(2)}) async-start(), calls=%async_computation.1 | async-start | bytes 2396160 | tf_op jit(solution)/shard_map/all_gather | solution.py:97
  12.0 465.7 %all-gather.17.cloned.1.call-start = ((), (), s32[]{:S(2)}) async-start(), calls=%async_computation.4 | async-start | bytes 2129920 | tf_op jit(solution)/shard_map/all_gather | solution.py:17
  12.1 1.3 copy-start.11
  67.1 200.2 %copy-start.2 = (bf16[8,144,64]{1,2,0:T(8,128)(2,1)}, bf16[8,144,64]{1,2,0:T(8,128)(2,1)S(1)}, u32[]{:S(2)}) copy-start(bf16[8,144,64]{1,2,0:T(8,128)(2,1)S(1)} %get-tuple-element.233) | copy-start | bytes 442372
  267.4 163.9 %copy-start.1 = (bf16[144,128]{1,0:T(8,128)(2,1)S(1)}, bf16[144,128]{1,0:T(8,128)(2,1)}, u32[]{:S(2)}) copy-start(bf16[144,128]{1,0:T(8,128)(2,1)} %param.13) | copy-start | bytes 110596
  329.9 102.6 %copy-start.12 = (bf16[144,1024]{1,0:T(8,128)(2,1)S(1)}, bf16[144,1024]{1,0:T(8,128)(2,1)}, u32[]{:S(2)}) copy-start(bf16[144,1024]{1,0:T(8,128)(2,1)} %param.11) | copy-start | bytes 884740
  329.9 103.8 %copy-start.3 = (bf16[8,144,64]{1,2,0:T(8,128)(2,1)S(1)}, bf16[8,144,64]{1,2,0:T(8,128)(2,1)}, u32[]{:S(2)}) copy-start(bf16[8,144,64]{1,2,0:T(8,128)(2,1)} %copy-done.2) | copy-start | bytes 442372
  332.7 196.6 %copy-start.6 = (f32[144]{0:T(256)S(1)}, f32[144]{0:T(256)}, u32[]{:S(2)}) copy-start(f32[144]{0:T(256)} %copy-done.5) | copy-start | bytes 1732
  332.7 196.6 %copy-start.8 = (f32[144]{0:T(256)S(1)}, f32[144]{0:T(256)}, u32[]{:S(2)}) copy-start(f32[144]{0:T(256)} %copy-done.7) | copy-start | bytes 1732
  332.7 196.6 %copy-start.10 = (f32[144]{0:T(256)S(1)}, f32[144]{0:T(256)}, u32[]{:S(2)}) copy-start(f32[144]{0:T(256)} %copy-done.9) | copy-start | bytes 1732
  332.9 196.5 %copy-start.4 = (bf16[144,128]{1,0:T(8,128)(2,1)S(1)}, bf16[144,128]{1,0:T(8,128)(2,1)}, u32[]{:S(2)}) copy-start(bf16[144,128]{1,0:T(8,128)(2,1)} %param.12) | copy-start | bytes 110596
  334.8 468.7 %all-reduce.2.cloned.1.call-start = ((), (), s32[]{:S(2)}) async-start(), calls=%async_computation.2 | async-start | bytes 524288 | tf_op jit(solution)/shard_map/psum | solution.py:196
Sparse Core Ops, SparseCore 0:
  11.6 88.1 all-gather.14
  102.9 80.7 all-gather.10
  186.7 80.5 all-gather.12
  334.9 80.1 all-gather.16
  477.2 147.5 all-reduce.1
where the time goes:
time: 818 us; the launch traced here: 813 us
  blocking collectives  462 us (56%)
  waiting for transfers between devices  200 us (24%)
  other arithmetic  73.9 us (9%)
  matrix products  53 us (6%)
  between operations  16.5 us (2%)
    psum x1, blocking collectives, local(): query_grad, key_grad = lax.psum((query_grad, key_grad), 'seq')  274 us
    psum x1, blocking collectives, local(): transfer_loss = lax.psum(loss_local, ('seq', 'head')) / seg_total  95.5 us
    all_gather x2, blocking collectives, prefix(): lax.all_gather(a.astype(kind), axis)  92.4 us
    all_gather x1, waiting for transfers between devices, local(): value_block = lax.all_gather(value_matrix, 'seq', axis=0, tiled=True)  83.7 us
    all_gather x1, waiting for transfers between devices, local(): key_block = lax.all_gather(key_matrix, 'seq', axis=0, tiled=True)  83.5 us
    add x126, other arithmetic, add_pair(): return (earlier_pair[0] + later_pair[0], earlier_pair[1] + later_pair[1])  49.7 us
    all_gather x2, waiting for transfers between devices, prefix(): lax.all_gather(a.astype(kind), axis)  31.2 us
    reduce_sum x1, other arithmetic, attend(): row_sum = jnp.sum(exponent, axis=-1)  21.9 us
  transfers between devices with their start and end apart: 5, of which 3 were waited for; matrix products, arithmetic and copies ran while one was open for 7% of the time, Pallas kernels for 0%

commit v1 on v0

--- a/solution.py
+++ b/solution.py
@@ -93,8 +93,13 @@
         )
 
     first_key = jnp.int32(0)
-    key_block = lax.all_gather(key_matrix, "seq", axis=0, tiled=True)
-    value_block = lax.all_gather(value_matrix, "seq", axis=0, tiled=True)
+    key_block, value_block = jnp.split(
+        lax.all_gather(
+            jnp.concatenate([key_matrix, value_matrix], axis=1), "seq", axis=0, tiled=True
+        ),
+        [key_matrix.shape[1]],
+        axis=1,
+    )
     key_count = key_block.shape[0]
     key_view = key_block.reshape(key_count, local_heads, HEAD_SIZE)
     value_view = value_block.reshape(key_count, local_heads, HEAD_SIZE)

time: 818 us -> 737 us (0.901)
  waiting for transfers between devices: 200 us -> 118 us
    all_gather x2 -> x1, waiting for transfers between devices: 167 us -> 87.2 us  [local(): lax.all_gather(jnp.concatenate([key_matrix, value_matrix], axis=1), 'seq'...]
  transfers between devices with their start and end apart: 5 -> 4, of which waited for: 3 -> 2; matrix products, arithmetic and copies ran while one was open for 7% -> 9% of each run, Pallas kernels for 0% -> 0%
where the time goes in v1:
time: 737 us; the launch traced here: 732 us
  blocking collectives  463 us (63%)
  waiting for transfers between devices  118 us (16%)
  other arithmetic  75.1 us (10%)
  matrix products  50.9 us (7%)
  between operations  16.5 us (2%)
    psum x1, blocking collectives, local(): query_grad, key_grad = lax.psum((query_grad, key_grad), 'seq')  274 us
    psum x1, blocking collectives, local(): transfer_loss = lax.psum(loss_local, ('seq', 'head')) / seg_total  95.5 us
    all_gather x2, blocking collectives, prefix(): lax.all_gather(a.astype(kind), axis)  93.2 us
    all_gather x1, waiting for transfers between devices, local(): lax.all_gather(jnp.concatenate([key_matrix, value_matrix], axis=1), 'seq'...  87.2 us
    add x126, other arithmetic, add_pair(): return (earlier_pair[0] + later_pair[0], earlier_pair[1] + later_pair[1])  49.8 us
    all_gather x2, waiting for transfers between devices, prefix(): lax.all_gather(a.astype(kind), axis)  31.1 us
    reduce_sum x1, other arithmetic, attend(): row_sum = jnp.sum(exponent, axis=-1)  21.5 us
    dot_general x1, matrix products, attend(): jnp.einsum('rkgd,lkd->kgrl', row_block, key_view, preferred_element_type=...  18.7 us
  transfers between devices with their start and end apart: 4, of which 2 were waited for; matrix products, arithmetic and copies ran while one was open for 9% of the time, Pallas kernels for 0%

profile of v1, /device:TPU:2, one launch (start us, length us, event | category | flops | bytes accessed | tf_op | source)
XLA Modules:
  0.0 731.8 jit_solution(14801025356595537953)
XLA Ops:
  7.9 0.9 fusion.101
  9.0 1.6 convolution_convert_fusion
  10.6 1.4 pad_maximum_fusion.1
  13.4 1.0 copy.51
  14.6 49.8 %all-gather.4 = bf16[64,1,128]{2,1,0:T(2,128)(2,1)S(1)} all-gather(bf16[1,1,128]{2,1,0:T(2,128)(2,1)S(1)} %bitcast.273), channel_id=3, replica_groups=mesh['seq'=64,'head'=8] {'seq'}, dimensions={0}, use_global_device_ids=true | all-gather | bytes 16640 | tf_op jit(solution)/shard_map/all_gather | solution.py:17
  64.4 1.3 fusion.105
  65.7 1.3 fusion.102
  67.6 1.1 fusion.40
  68.7 31.1 %all-gather.12.cloned.1.call-done = bf16[8192,128]{1,0:T(8,128)(2,1)} async-done(((bf16[128,128]{1,0:T(8,128)(2,1)}), bf16[8192,128]{1,0:T(8,128)(2,1)}) %all-gather.12.cloned.1.call-update) | async-done | bytes 2097168 | tf_op jit(solution)/shard_map/all_gather | solution.py:17
  100.2 87.2 %all-gather.10.cloned.1.call-done = bf16[9216,256]{1,0:T(8,128)(2,1)} async-done(((bf16[144,256]{1,0:T(8,128)(2,1)}), bf16[9216,256]{1,0:T(8,128)(2,1)}) %all-gather.10.cloned.1.call-update) | async-done | bytes 4718608 | tf_op jit(solution)/shard_map/all_gather | solution.py:97
  187.4 58.2 %conditional.1 = (f32[1,8,144]{2,1,0:T(8,128)S(1)}, f32[1,8,144,128]{3,2,1,0:T(8,128)S(1)}) conditional(s32[]{:T(128)} %bitcast.28, () %tuple.33, (s32[9216]{0:T(1024)S(1)}, s32[144]{0:T(256)S(1)}, bf16[9216,256]{1,0:T(8,128)(2,1)}, bf16[144,1024]{1,0:T(8,128)(2,1)}) %tuple.34), branch_computations={%region_12.13_spmd, %region_13.16_spmd} | conditional | flops 5575162880 | bytes 157256816 | solution.py:118
  188.4 18.7 %fusion = (f32[8,144]{1,0:T(8,128)S(1)}, f32[9216,144,8]{0,1,2:T(8,128)}) fusion(pred[144,9216]{1,0:T(8,128)(4,1)S(1)} %broadcast_compare_fusion, bf16[9216,256]{1,0:T(8,128)(2,1)} %get-tuple-element.119, bf16[144,1024]{1,0:T(8,128)(2,1)} %get-tuple-element.120), kind=kOutput, calls=%fused_computation.4 | convolution fusion | flops 2749758464 | bytes 46453248 | tf_op jit(solution)/shard_map/cond/branch_1_fun/rkgd,lkd->kgrl/dot_general | solution.py:57
  207.1 21.5 %fusion.2 = f32[8,144]{1,0:T(8,128)S(1)} fusion(f32[9216,144,8]{0,1,2:T(8,128)} %get-tuple-element.217, f32[8,144]{1,0:T(8,128)S(1)} %broadcast_maximum_fusion, pred[144,9216]{1,0:T(8,128)(4,1)S(1)} %broadcast_compare_fusion), kind=kLoop, calls=%fused_computation.6 | loop fusion | flops 53083008 | bytes 43803648 | tf_op jit(solution)/shard_map/cond/branch_1_fun/reduce_sum | solution.py:66
  228.7 17.0 %fusion.12 = f32[1,8,144,128]{3,2,1,0:T(8,128)S(1)} fusion(bf16[9216,256]{1,0:T(8,128)(2,1)S(1)} %copy-done.15, f32[9216,144,8]{0,1,2:T(8,128)} %get-tuple-element.217, f32[8,144]{1,0:T(8,128)S(1)} %broadcast_maximum_fusion, pred[144,9216]{1,0:T(8,128)(4,1)S(1)} %broadcast_compare_fusion), kind=kOutput, calls=%fused_computation.16 | convolution fusion | flops 2770993152 | bytes 46751744 | tf_op jit(solution)/shard_map/cond/branch_1_fun/kgrl,lkd->kgrd/dot_general | solution.py:65
  246.3 2.4 multiply_reduce_fusion
  248.9 0.9 fusion.36
  249.9 95.5 %psum.23 = f32[]{:T(128)} all-reduce(f32[]{:T(128)} %get-tuple-element.183), channel_id=1, replica_groups=mesh['seq'=64,'head'=8] {'seq','head'}, use_global_device_ids=true, to_apply=%region_26.27 | all-reduce | flops 1 | bytes 8 | tf_op jit(solution)/shard_map/psum | solution.py:202
  347.0 1.1 fusion.27
  348.4 1.1 fusion.26
  349.7 1.3 fusion.47
  351.0 0.8 copy.65
  352.3 43.4 %all-gather.5 = bf16[64,1,128]{2,1,0:T(2,128)(2,1)S(1)} all-gather(bf16[1,1,128]{2,1,0:T(2,128)(2,1)S(1)} %fusion.38), channel_id=5, replica_groups=mesh['seq'=64,'head'=8] {'seq'}, dimensions={0}, use_global_device_ids=true | all-gather | bytes 16640 | tf_op jit(solution)/shard_map/all_gather | solution.py:17
  396.8 51.3 %while.27 = (s32[]{:T(128)}, f32[1,128,128]{2,1,0:T(8,128)S(1)}, f32[1,128]{1,0:T(1,128)S(1)}, s32[]{:T(128)}, bf16[64,1,128,128]{3,2,1,0:T(8,128)(2,1)}, /*inde...) while((s32[]{:T(128)}, f32[1,128,128]{2,1,0:T(8,128)S(1)}, ...), condition=%wide.region_21.22_spmd, body=%wide.region_20.21_spmd.sunk | while | flops 33030 | bytes 165283 | solution.py:32
  402.5 0.8 convert_add_fusion.10
  403.3 0.8 convert_add_fusion.10
  409.0 0.8 convert_add_fusion.10
  409.8 0.8 convert_add_fusion.10
  413.1 0.8 convert_add_fusion.10
  413.9 0.8 convert_add_fusion.10
  414.7 0.8 convert_add_fusion.10
  448.5 274.0 %psum.22 = f32[128,64]{0,1:T(8,128)} all-reduce(f32[128,64]{0,1:T(8,128)S(1)} %convolution_bitcast_fusion.3), channel_id=1, replica_groups=mesh['seq'=64,'head'=8] {'seq'}, use_global_device_ids=true, to_apply=%region_24.25 | all-reduce | flops 8192 | bytes 65536 | tf_op jit(solution)/shard_map/psum | solution.py:201
  722.5 1.7 copy.144
  (191 shorter events, 51.9 us)
Async XLA Ops:
  7.2 0.7 copy-start
  7.2 92.6 %all-gather.12.cloned.1.call-start = ((), (), s32[]{:S(2)}) async-start(), calls=%async_computation.2 | async-start | bytes 2129920 | tf_op jit(solution)/shard_map/all_gather | solution.py:17
  8.8 4.5 copy-start.6
  8.8 4.5 copy-start.8
  8.9 4.5 copy-start.10
  8.9 4.5 copy-start.12
  9.0 90.9 %copy-start.4 = (bf16[144,64]{0,1:T(8,128)(2,1)}, bf16[144,64]{0,1:T(8,128)(2,1)S(1)}, u32[]{:S(2)}) copy-start(bf16[144,64]{0,1:T(8,128)(2,1)S(1)} %get-tuple-element.222) | copy-start | bytes 55300
  9.0 178.5 %copy-start.3 = (bf16[144,64]{0,1:T(8,128)(2,1)}, bf16[144,64]{0,1:T(8,128)(2,1)S(1)}, u32[]{:S(2)}) copy-start(bf16[144,64]{0,1:T(8,128)(2,1)S(1)} %get-tuple-element.219) | copy-start | bytes 55300
  10.6 176.9 %all-gather.10.cloned.1.call-start = ((), (), s32[]{:S(2)}) async-start(), calls=%async_computation | async-start | bytes 4792320 | tf_op jit(solution)/shard_map/all_gather | solution.py:97
  12.1 384.7 %all-gather.14.cloned.1.call-start = ((), (), s32[]{:S(2)}) async-start(), calls=%async_computation.3 | async-start | bytes 2129920 | tf_op jit(solution)/shard_map/all_gather | solution.py:17
  64.4 3.2 copy-start.5
  187.4 159.5 %copy-start.1 = (bf16[144,128]{1,0:T(8,128)(2,1)S(1)}, bf16[144,128]{1,0:T(8,128)(2,1)}, u32[]{:S(2)}) copy-start(bf16[144,128]{1,0:T(8,128)(2,1)} %param.13) | copy-start | bytes 110596
  207.1 21.5 %copy-start.15 = (bf16[9216,256]{1,0:T(8,128)(2,1)S(1)}, bf16[9216,256]{1,0:T(8,128)(2,1)}, u32[]{:S(2)}) copy-start(bf16[9216,256]{1,0:T(8,128)(2,1)} %get-tuple-element.119) | copy-start | bytes 14155780 | tf_op jit(solution)/shard_map/cond
  245.7 0.6 copy-start.14
  248.6 199.6 %copy-start.7 = (f32[144]{0:T(256)S(1)}, f32[144]{0:T(256)}, u32[]{:S(2)}) copy-start(f32[144]{0:T(256)} %copy-done.6) | copy-start | bytes 1732
  248.6 199.6 %copy-start.9 = (f32[144]{0:T(256)S(1)}, f32[144]{0:T(256)}, u32[]{:S(2)}) copy-start(f32[144]{0:T(256)} %copy-done.8) | copy-start | bytes 1732
  248.6 199.6 %copy-start.11 = (f32[144]{0:T(256)S(1)}, f32[144]{0:T(256)}, u32[]{:S(2)}) copy-start(f32[144]{0:T(256)} %copy-done.10) | copy-start | bytes 1732
  248.6 199.7 %copy-start.13 = (f32[144]{0:T(256)S(1)}, f32[144]{0:T(256)}, u32[]{:S(2)}) copy-start(f32[144]{0:T(256)} %copy-done.12) | copy-start | bytes 1732
  248.9 199.5 %copy-start.2 = (bf16[144,128]{1,0:T(8,128)(2,1)S(1)}, bf16[144,128]{1,0:T(8,128)(2,1)}, u32[]{:S(2)}) copy-start(bf16[144,128]{1,0:T(8,128)(2,1)} %param.12) | copy-start | bytes 110596
  249.8 472.6 %all-reduce.2.cloned.1.call-start = ((), (), s32[]{:S(2)}) async-start(), calls=%async_computation.1 | async-start | bytes 524288 | tf_op jit(solution)/shard_map/psum | solution.py:201
Sparse Core Ops, SparseCore 0:
  11.6 88.1 all-gather.11
  103.4 83.9 all-gather.9
  250.0 80.2 all-gather.13
  396.2 147.4 all-reduce.1
